TPU v7x, 32 devices: a whole 2x2x4 slice. The times are simulated.
32 devices in a mesh: row: 2 (over x), col: 4 (over z), box: 4 (over y, core).
Axes of the slice: x: 2, y: 2, z: 4, core: 2. Of those that a mesh axis runs over, the one named last changes fastest.
Arguments:
- coeffs: bfloat16 [81920, 512], P(('row', 'box'), 'col'), may hold values from -6 to 6
- reflectors: bfloat16 [81920, 256], P(('row', 'box')), may hold values from -0.078125 to 0.078125
- factor: float32 [256, 256], replicated, may hold values from -0.375 to 0.375
- func_exp: float32 [81920], replicated, may hold values from 0.5 to 20
- func_atom: int32 [81920], replicated, may hold values from 0 to 8191, never falling along the last dimension, each value on 1 to 20 neighbouring positions
- atom_pos: float32 [3, 8192], replicated, may hold values from 0 to 1
- point_pos: float32 [3, 128, 128], P(None, ('row', 'col', 'box')), may hold values from 0 to 1
- send_tiles: int32 [8, 8, 2], replicated, may hold values from 0 to 79, as said below
- box_tiles: int32 [128, 16], P(('row', 'col', 'box')), may hold values from 0 to 15, as said below
- box_count: int32 [128], P(('row', 'col', 'box')), may hold values from 1 to 16
Outputs:
- rotated: bfloat16 [81920, 512], P(('row', 'box'), 'col')
- density: float32 [128, 128], P(('row', 'col', 'box'))
Inputs may be any that keep to these rules, and one draw needn't show every extreme that they name: `send_tiles`: for each basis group and box group the 2 tiles are different local tiles of the basis group. `box_tiles`: the 16 slots listed by a box are different. `func_atom`: never falls along the basis functions; every atom carries 1 to 20 functions.
All inputs are finite; a program needn't handle non-finite values.
Results may differ from a plain program's by a relative error of at most 0.015.
Values may be sent and summed in bfloat16 or wider, within the bound.
A program may use at most 128 MiB of HBM per device.

v0:
```python
import math

import jax
import jax.numpy as jnp
from jax import lax
from jax.sharding import PartitionSpec as P

K = 512
TILE = 128


def box_density(arrived, slot_alpha, slot_centre, listed, count, points):
    alpha = slot_alpha[listed]
    centre = slot_centre[:, listed]
    first = points[0][:, None, None] - centre[0][None]
    dist = first * first
    second = points[1][:, None, None] - centre[1][None]
    dist = dist + second * second
    third = points[2][:, None, None] - centre[2][None]
    dist = dist + third * third
    live = jnp.arange(listed.shape[0], dtype=jnp.int32) < count
    phi = jnp.where(live[None, :, None], jnp.exp(-alpha[None] * dist), 0.0).astype(jnp.bfloat16)
    phi = phi.reshape(points.shape[1], -1)
    block = arrived[listed].reshape(-1, arrived.shape[2])
    orbital = jnp.dot(phi, block, preferred_element_type=jnp.float32)
    return jnp.sum(orbital * orbital, 1) / (K * TILE)


def by_blocks(arrived, slot_alpha, slot_centre, lists, counts, points):
    boxes = lists.shape[0]
    width = math.gcd(boxes, 2)
    steps = boxes // width
    lists_blocked = lists.reshape(steps, width, lists.shape[1])
    counts_blocked = counts.reshape(steps, width)
    moved = jnp.moveaxis(points, 1, 0)
    points_blocked = moved.reshape(steps, width, moved.shape[1], moved.shape[2])
    single = jax.vmap(
        lambda listed, count, where: box_density(
            arrived, slot_alpha, slot_centre, listed, count, where
        )
    )

    def one_block(items):
        return single(items[0], items[1], items[2])

    result = lax.map(one_block, (lists_blocked, counts_blocked, points_blocked))
    return result.reshape(boxes, result.shape[2])


def per_device(
    coeffs,
    reflectors,
    factor,
    func_exp,
    func_atom,
    atom_pos,
    point_pos,
    send_tiles,
    box_tiles,
    box_count,
):
    panel_part = jnp.dot(reflectors.T, coeffs, preferred_element_type=jnp.float32)
    panel = lax.psum(panel_part.astype(jnp.bfloat16), ("row", "box")).astype(jnp.float32)
    scaled = jnp.dot(factor, panel, precision=lax.Precision.HIGHEST).astype(jnp.bfloat16)
    rotated = (
        coeffs.astype(jnp.float32) - jnp.dot(reflectors, scaled, preferred_element_type=jnp.float32)
    ).astype(jnp.bfloat16)
    peers = lax.axis_size(("row", "box"))
    group = lax.axis_index(("row", "box"))
    capacity = send_tiles.shape[2]
    local_tiles = coeffs.shape[0] // TILE
    slots = jnp.arange(peers * capacity, dtype=jnp.int32)
    source = slots // capacity
    within = slots % capacity
    tile = source * local_tiles + send_tiles[source, group, within]
    funcs = tile[:, None] * TILE + jnp.arange(TILE, dtype=jnp.int32)[None, :]
    slot_alpha = func_exp[funcs]
    slot_centre = atom_pos[:, func_atom[funcs]]
    outgoing_index = send_tiles[group]
    outgoing = rotated.reshape(local_tiles, TILE, rotated.shape[1])[outgoing_index]
    arrived = lax.all_to_all(outgoing, ("row", "box"), split_axis=0, concat_axis=0, tiled=True)
    arrived = arrived.reshape(peers * capacity, TILE, arrived.shape[3])
    lists, counts = (
        lax.all_gather(box_tiles, "col", axis=0, tiled=True),
        lax.all_gather(box_count, "col", axis=0, tiled=True),
    )
    points = lax.all_gather(point_pos, "col", axis=1, tiled=True)
    partial_value = by_blocks(arrived, slot_alpha, slot_centre, lists, counts, points)
    density = lax.psum_scatter(
        partial_value.astype(jnp.bfloat16), "col", scatter_dimension=0, tiled=True
    ).astype(jnp.float32)
    return (rotated, density)


def solution(mesh):
    in_specs = (
        P(("row", "box"), "col"),
        P(("row", "box"), None),
        P(),
        P(),
        P(),
        P(),
        P(None, ("row", "col", "box"), None),
        P(),
        P(("row", "col", "box"), None),
        P(("row", "col", "box")),
    )
    out_specs = (P(("row", "box"), "col"), P(("row", "col", "box"), None))
    return jax.shard_map(
        per_device, mesh=mesh, in_specs=in_specs, out_specs=out_specs, check_vma=False
    )
```

profile of v0, /device:TPU:0, one launch (start us, length us, event | category | flops | bytes accessed | tf_op | source)
XLA Modules:
  0.0 196.5 jit_solution(6431484893824231304)
XLA Ops:
  7.2 5.5 %convolution_convert_fusion = bf16[256,128]{1,0:T(8,128)(2,1)} fusion(bf16[10240,256]{1,0:T(8,128)(2,1)} %param.13, bf16[10240,128]{1,0:T(8,128)(2,1)} %param.12), kind=kOutput, calls=%fused_computation.42 | convolution fusion | flops 671121408 | bytes 7929856 | tf_op jit(solution)/shard_map/dot_general | solution.py:62
  13.8 3.0 %copy.28 = bf16[10240,128]{0,1:T(8,128)(2,1)S(1)} copy(bf16[10240,128]{1,0:T(8,128)(2,1)} %param.12) | data formatting | bytes 5242880 | tf_op args[0]
  16.8 2.6 %copy.31 = f32[3,8192]{0,1:T(8,128)} copy(f32[3,8192]{1,0:T(4,128)S(1)} %copy-done.5) | data formatting | bytes 196608 | tf_op args[5]
  19.4 48.7 %all-reduce.4.cloned.1.call-done = bf16[256,128]{1,0:T(8,128)(2,1)} async-done(((bf16[256,128]{1,0:T(8,128)(2,1)}), bf16[256,128]{1,0:T(8,128)(2,1)}) %all-reduce.4.cloned.1.call-update) | async-done | bytes 65552 | tf_op jit(solution)/shard_map/psum | solution.py:63
  68.1 1.1 convolution_convert_fusion.1
  69.3 5.8 %fusion.13 = bf16[10240,128]{0,1:T(8,128)(2,1)} fusion(bf16[128,256]{1,0:T(8,128)(2,1)S(1)} %convolution_convert_fusion.1, bf16[10240,256]{1,0:T(8,128)(2,1)} %param.13, bf16[10240,128]{0,1:T(8,128)(2,1)S(1)} %copy.28), kind=kOutput, calls=%fused_computation.41 | convolution fusion | flops 675020800 | bytes 10551296 | tf_op jit(solution)/shard_map/dot_general | solution.py:66
  75.1 3.2 %copy.36 = bf16[10240,128]{1,0:T(8,128)(2,1)S(1)} copy(bf16[10240,128]{0,1:T(8,128)(2,1)} %fusion.13) | data formatting | bytes 5242880
  78.3 1.6 gather_fusion.7
  80.0 3.5 %all-to-all-start = ((bf16[8,2,128,128]{3,2,1,0:T(8,128)(2,1)}), bf16[8,2,128,128]{3,2,1,0:T(8,128)(2,1)S(1)}, u32[]{:S(2)}, u32[]{:S(2)}) async-start(bf16[8,2,128,128]{3,2,1,0:T(8,128)(2,1)} %bitcast.116), calls=%async_computation | async-start | bytes 1048576 | tf_op jit(solution)/shard_map/all_to_all | solution.py:81
  83.6 11.8 %gather_fusion.5 = s32[2048]{0:T(1024)S(1)} fusion(s32[81920]{0:T(1024)S(1)} %copy-done, s32[2048]{0:T(1024)S(1)} %fusion.15), kind=kCustom, calls=%fused_computation.5 | custom fusion | bytes 24576 | tf_op jit(solution)/shard_map/gather | solution.py:78
  95.4 7.7 %gather_fusion.6 = f32[2048,3]{1,0:T(8,128)S(1)} fusion(f32[3,8192]{0,1:T(8,128)} %copy.31, s32[2048]{0:T(1024)S(1)} %fusion.17), kind=kCustom, calls=%fused_computation.6 | custom fusion | bytes 57344 | tf_op jit(solution)/shard_map/gather | solution.py:78
  103.4 11.8 %gather_fusion.4 = f32[2048]{0:T(1024)S(1)} fusion(f32[81920]{0:T(1024)S(1)} %copy-done.1, s32[2048]{0:T(1024)S(1)} %fusion.15), kind=kCustom, calls=%fused_computation.4 | custom fusion | bytes 24576 | tf_op jit(solution)/shard_map/gather | solution.py:77
  116.8 8.3 %all-reduce = s32[16]{0:T(128)S(1)} all-reduce(s32[16]{0:T(128)S(1)} %dynamic-update-slice), channel_id=1, replica_groups=mesh['row'=2,'col'=4,'box'=4] {'col'}, use_global_device_ids=true, to_apply=%add | all-reduce | flops 16 | bytes 128
  125.1 13.1 %all_gather.11 = f32[3,16,128]{2,0,1:T(4,128)S(1)} all-gather(f32[3,4,128]{2,0,1:T(4,128)S(1)} %copy.29), channel_id=1, replica_groups=mesh['row'=2,'col'=4,'box'=4] {'col'}, dimensions={1}, use_global_device_ids=true | all-gather | bytes 30720 | tf_op jit(solution)/shard_map/all_gather | solution.py:87
  138.9 11.9 %all-gather = s32[4,4,16]{2,1,0:T(4,128)S(1)} all-gather(s32[1,4,16]{2,1,0:T(4,128)S(1)} %bitcast.126), channel_id=1, replica_groups=mesh['row'=2,'col'=4,'box'=4] {'col'}, dimensions={0}, use_global_device_ids=true | all-gather | bytes 1280 | tf_op jit(solution)/shard_map/all_gather | solution.py:84
  150.8 29.7 %while.10 = (s32[]{:T(128)}, bf16[8,2,128]{2,1,0:T(2,128)(2,1)S(1)}, s32[8,2]{1,0:T(8,128)S(1)}, s32[8,2,16]{2,1,0:T(2,128)S(1)}, f32[16,128]{1,0:T(8,128)S(1)},...) while((s32[]{:T(128)}, ...), condition=%wide.region_3.4_spmd, body=%wide.region_1.3_spmd.sunk | while | flops 140055680 | bytes 3644613 | solution.py:46
  151.7 0.7 gather_fusion
  153.3 1.2 fusion.41
  155.4 0.7 gather_fusion
  157.0 1.2 fusion.41
  159.1 0.7 gather_fusion
  160.7 1.2 fusion.41
  162.8 0.7 gather_fusion
  164.4 1.2 fusion.41
  166.5 0.7 gather_fusion
  168.1 1.2 fusion.41
  170.3 0.7 gather_fusion
  171.8 1.2 fusion.41
  174.0 0.7 gather_fusion
  175.5 1.2 fusion.41
  179.3 1.2 fusion.41
  180.5 8.6 %all-reduce.1 = bf16[16,128]{1,0:T(8,128)(2,1)S(1)} all-reduce(bf16[16,128]{1,0:T(8,128)(2,1)S(1)} %bitcast.125), channel_id=2, replica_groups=mesh['row'=2,'col'=4,'box'=4] {'col'}, use_global_device_ids=true, to_apply=%region_4.5.clone | all-reduce | flops 2048 | bytes 8192
  (178 shorter events, 17.0 us)
Async XLA Ops:
  7.2 76.4 %copy-start = (s32[81920]{0:T(1024)S(1)}, s32[81920]{0:T(1024)}, u32[]{:S(2)}) copy-start(s32[81920]{0:T(1024)} %param.16) | copy-start | bytes 983044
  7.2 5.7 %copy-start.2 = (s32[8,8,2]{1,2,0:T(2,128)S(1)}, s32[8,8,2]{1,2,0:T(2,128)}, u32[]{:S(2)}) copy-start(s32[8,8,2]{1,2,0:T(2,128)} %param.19) | copy-start | bytes 1540
  7.2 60.9 %all-reduce.4.cloned.1.call-start = ((), (), s32[]{:S(2)}) async-start(), calls=%async_computation.1 | async-start | bytes 131072 | tf_op jit(solution)/shard_map/psum | solution.py:63
  13.7 3.1 %copy-start.5 = (f32[3,8192]{1,0:T(4,128)S(1)}, f32[3,8192]{1,0:T(4,128)}, u32[]{:S(2)}) copy-start(f32[3,8192]{1,0:T(4,128)} %param.17) | copy-start | bytes 294916
  16.8 51.3 %copy-start.4 = (f32[256,256]{1,0:T(8,128)S(1)}, f32[256,256]{1,0:T(8,128)}, u32[]{:S(2)}) copy-start(f32[256,256]{1,0:T(8,128)} %param.14) | copy-start | bytes 786436
  78.3 5.2 %copy-start.3 = (bf16[10240,128]{1,0:T(8,128)(2,1)}, bf16[10240,128]{1,0:T(8,128)(2,1)S(1)}, u32[]{:S(2)}) copy-start(bf16[10240,128]{1,0:T(8,128)(2,1)S(1)} %copy.36) | copy-start | bytes 7864324
  80.0 70.8 %all-to-all-start = ((bf16[8,2,128,128]{3,2,1,0:T(8,128)(2,1)}), bf16[8,2,128,128]{3,2,1,0:T(8,128)(2,1)S(1)}, u32[]{:S(2)}, u32[]{:S(2)}) async-start(bf16[8,2,128,128]{3,2,1,0:T(8,128)(2,1)} %bitcast.116), calls=%async_computation | async-start | bytes 1048576 | tf_op jit(solution)/shard_map/all_to_all | solution.py:81
  95.4 8.1 %copy-start.1 = (f32[81920]{0:T(1024)S(1)}, f32[81920]{0:T(1024)}, u32[]{:S(2)}) copy-start(f32[81920]{0:T(1024)} %param.15) | copy-start | bytes 983044
  103.4 11.8 %copy-start.8 = (u32[32]{0:T(128)S(1)}, u32[32]{0:T(128)}, u32[]{:S(2)}) copy-start(u32[32]{0:T(128)} %constant.107) | copy-start | bytes 388
  103.4 13.1 %copy-start.9 = (s32[4]{0:T(128)S(1)}, s32[4]{0:T(128)}, u32[]{:S(2)}) copy-start(s32[4]{0:T(128)} %param.21) | copy-start | bytes 52
  103.4 21.7 %copy-start.6 = (f32[3,4,128]{2,1,0:T(4,128)S(1)}, f32[3,4,128]{2,1,0:T(4,128)}, u32[]{:S(2)}) copy-start(f32[3,4,128]{2,1,0:T(4,128)} %param.18) | copy-start | bytes 18436
  103.4 35.5 %copy-start.7 = (s32[4,16]{1,0:T(4,128)S(1)}, s32[4,16]{1,0:T(4,128)}, u32[]{:S(2)}) copy-start(s32[4,16]{1,0:T(4,128)} %param.20) | copy-start | bytes 772
Sparse Core Ops, SparseCore 0:
  12.9 55.1 all-reduce.3
where the time goes:
time: 197 us
  local copies, waits for them, and re-layouts  62.4 us (32%)
  waiting for transfers between devices  48.7 us (25%)
  blocking collectives  41.9 us (21%)
  matrix products  22.2 us (11%)
  between operations  15.6 us (8%)
  starting transfers between devices  3.53 us (2%)
    psum x1, waiting for transfers between devices, per_device(): lax.psum(panel_part.astype(jnp.bfloat16), ('row', 'box'))  48.7 us
    gather x3, local copies, waits for them, and re-layouts, per_device(): slot_centre = atom_pos[:, func_atom[funcs]]  19.8 us
    unnamed x2, blocking collectives  16.9 us
    all_gather x1, blocking collectives, per_device(): points = lax.all_gather(point_pos, 'col', axis=1, tiled=True)  13.1 us
    all_gather x1, blocking collectives, per_device(): lax.all_gather(box_tiles, 'col', axis=0, tiled=True)  11.9 us
    gather x1, local copies, waits for them, and re-layouts, per_device(): slot_alpha = func_exp[funcs]  11.8 us
    unnamed x27, local copies, waits for them, and re-layouts  9.83 us
    dot_general x8, matrix products, box_density(): orbital = jnp.dot(phi, block, preferred_element_type=jnp.float32)  9.66 us
  transfers between devices with their start and end apart: 2, of which 1 were waited for; matrix products, arithmetic and copies ran while one was open for 20% of the time, Pallas kernels for 0%

commit v1 on v0

--- a/solution.py
+++ b/solution.py
@@ -1,8 +1,11 @@
+import functools
 import math
 
 import jax
 import jax.numpy as jnp
 from jax import lax
+from jax.experimental import pallas as pl
+from jax.experimental.pallas import tpu as pltpu
 from jax.sharding import PartitionSpec as P
 
 K = 512
@@ -47,7 +50,7 @@
     return result.reshape(boxes, result.shape[2])
 
 
-def per_device(
+def general(
     coeffs,
     reflectors,
     factor,
@@ -92,6 +95,467 @@
     return (rotated, density)
 
 
+MESH = pl.DeviceIdType.MESH
+LANES = 128
+LOAD = 1024
+EMIT = 1024
+
+
+def prepare(
+    n_box, coeffs_hbm, refl_hbm, alpha_ref, atom_ref, pos_ref, point_ref, send_ref, list_ref,
+    count_ref, slot_info, info_ref, picked_c, picked_r, window, pick_sem
+):
+    f32 = jnp.float32
+    me = lax.axis_index("row") * n_box + lax.axis_index("box")
+    slots, capacity = slot_info.shape[0], send_ref.shape[2]
+    boxes = list_ref.shape[0]
+    tiles = coeffs_hbm.shape[0] // TILE
+
+    def picks(s):
+        tile = send_ref[me, s // capacity, s % capacity]
+        source = pl.ds(pl.multiple_of(tile * TILE, TILE), TILE)
+        target = pl.ds(s * TILE, TILE)
+        return (
+            pltpu.make_async_copy(coeffs_hbm.at[source], picked_c.at[target], pick_sem.at[2 * s]),
+            pltpu.make_async_copy(refl_hbm.at[source], picked_r.at[target], pick_sem.at[2 * s + 1]),
+        )
+
+    for s in range(slots):
+        for copy in picks(s):
+            copy.start()
+
+    lane = lax.broadcasted_iota(jnp.int32, (1, LANES), 1)
+    info = [point_ref[c] for c in range(3)]
+    for b in range(boxes):
+        live = jnp.zeros((1, LANES), f32)
+        for i in range(list_ref.shape[1]):
+            used = jnp.where(i < count_ref[b], list_ref[b, i], -1)
+            live = jnp.where(lane == used, 1.0, live)
+        info.append(live)
+    info_ref[...] = jnp.concatenate(info, axis=0)
+
+    window[...] = jnp.zeros_like(window)
+    last = pos_ref.shape[1] // LANES - 1
+    depth = lax.broadcasted_iota(jnp.int32, (2 * LANES, LANES), 0)
+
+    for s in range(slots):
+        q, j = s // capacity, s % capacity
+        tile = q * tiles + send_ref[q, me, j]
+        atoms = atom_ref[pl.ds(tile, 1), :]
+        block = jnp.min(atoms) // LANES
+        after = jnp.minimum(block + 1, last)
+        window[s, 0:3, 0:LANES] = pos_ref[:, pl.ds(pl.multiple_of(block * LANES, LANES), LANES)]
+        window[s, 0:3, LANES:] = pos_ref[:, pl.ds(pl.multiple_of(after * LANES, LANES), LANES)]
+        pick = jnp.where(depth == atoms - block * LANES, 1.0, 0.0)
+        slot_info[s, 0:8, :] = jnp.dot(
+            window[s], pick, precision=lax.Precision.HIGHEST, preferred_element_type=f32
+        )
+        slot_info[s, 3:4, :] = -alpha_ref[pl.ds(tile, 1), :]
+
+    for s in range(slots):
+        for copy in picks(s):
+            copy.wait()
+
+
+def kernel(
+    n_row,
+    n_box,
+    n_col,
+    coeffs_hbm,
+    refl_hbm,
+    factor_ref,
+    slot_info,
+    info_ref,
+    picked_c,
+    picked_r,
+    rot_hbm,
+    dens_ref,
+    coeffs_v,
+    refl_v,
+    rot_v,
+    part_f,
+    part_b,
+    got1,
+    scaled_t,
+    outbox,
+    arrived,
+    box_info,
+    planes,
+    phi,
+    dens_own,
+    dens_got,
+    load_sem,
+    emit_sem,
+    info_send,
+    info_recv,
+    sum_send,
+    sum_recv,
+    gather_send,
+    gather_recv,
+    tile_send,
+    tile_recv,
+    dens_send,
+    dens_recv,
+):
+    f32, bf16 = jnp.float32, jnp.bfloat16
+    peers = n_row * n_box
+    row, box, col = lax.axis_index("row"), lax.axis_index("box"), lax.axis_index("col")
+    me = row * n_box + box
+    rows, width = coeffs_v.shape
+    loads = rows // LOAD
+    emits = rows // EMIT
+    share = width // peers
+    slots = slot_info.shape[0]
+    capacity = slots // peers
+    boxes = dens_ref.shape[0]
+
+    def load(i):
+        at = pl.ds(i * LOAD, LOAD)
+        return (
+            pltpu.make_async_copy(coeffs_hbm.at[at], coeffs_v.at[at], load_sem.at[2 * i]),
+            pltpu.make_async_copy(refl_hbm.at[at], refl_v.at[at], load_sem.at[2 * i + 1]),
+        )
+
+    for i in range(loads):
+        for copy in load(i):
+            copy.start()
+
+    def in_plane(d):
+        peer = lax.rem(me + d, peers)
+        return peer, {"row": peer // n_box, "box": lax.rem(peer, n_box)}
+
+    def in_col(d):
+        peer = lax.rem(col + d, n_col)
+        return peer, {"col": peer}
+
+    barrier = pltpu.get_barrier_semaphore()
+    for d in range(1, peers):
+        pl.semaphore_signal(barrier, inc=1, device_id=in_plane(d)[1], device_id_type=MESH)
+    for d in range(1, n_col):
+        pl.semaphore_signal(barrier, inc=1, device_id=in_col(d)[1], device_id_type=MESH)
+
+    mine = pl.ds(pl.multiple_of(col * 16, 16), 16)
+    box_info[mine, :] = info_ref[...]
+
+    pl.semaphore_wait(barrier, peers - 1 + n_col - 1)
+
+    info_copies = []
+    for d in range(1, n_col):
+        copy = pltpu.make_async_remote_copy(
+            src_ref=box_info.at[mine],
+            dst_ref=box_info.at[mine],
+            send_sem=info_send.at[d],
+            recv_sem=info_recv.at[d],
+            device_id=in_col(d)[1],
+            device_id_type=MESH,
+        )
+        copy.start()
+        info_copies.append(copy)
+
+    part_f[...] = jnp.zeros_like(part_f)
+
+    @pl.loop(0, loads)
+    def _(i):
+        for copy in load(i):
+            copy.wait()
+        at = pl.ds(pl.multiple_of(i * LOAD, LOAD), LOAD)
+        part_f[...] += lax.dot_general(
+            coeffs_v[at, :], refl_v[at, :], (((0,), (0,)), ((), ())), preferred_element_type=f32
+        )
+
+    part_b[...] = part_f[...].astype(bf16)
+    sum_copies = []
+    for d in range(1, peers):
+        peer, where = in_plane(d)
+        copy = pltpu.make_async_remote_copy(
+            src_ref=part_b.at[pl.ds(pl.multiple_of(peer * share, share), share)],
+            dst_ref=got1.at[d],
+            send_sem=sum_send.at[d],
+            recv_sem=sum_recv.at[d],
+            device_id=where,
+            device_id_type=MESH,
+        )
+        copy.start()
+        sum_copies.append(copy)
+
+    for copy in info_copies:
+        copy.wait()
+    turned = jnp.concatenate(
+        [box_info[...], jnp.zeros((LANES - box_info.shape[0], LANES), f32)], axis=0
+    ).T
+    for j in range(n_col):
+        for b in range(boxes):
+            for c in range(4):
+                k = j * 16 + c * boxes + b
+                planes[j * boxes + b, c] = jnp.broadcast_to(turned[:, k : k + 1], (LANES, LANES))
+
+    def fill(first, count):
+        @pl.loop(first, first + count)
+        def _(n):
+            at = pl.ds(pl.multiple_of(n * LANES, LANES), LANES)
+
+            @pl.loop(0, slots)
+            def _(s):
+                one = planes[n, 0] - slot_info[s, 0:1, :]
+                dist = one * one
+                two = planes[n, 1] - slot_info[s, 1:2, :]
+                dist = dist + two * two
+                three = planes[n, 2] - slot_info[s, 2:3, :]
+                dist = dist + three * three
+                value = jnp.exp(slot_info[s, 3:4, :] * dist)
+                value = jnp.where(planes[n, 3, pl.ds(s, 1), :] > 0.0, value, 0.0)
+                phi[at, pl.ds(pl.multiple_of(s * LANES, LANES), LANES)] = value.astype(bf16)
+
+    fill(0, FILLS[0])
+
+    own = pl.ds(pl.multiple_of(me * share, share), share)
+    total = part_f[own, :]
+    for d in range(1, peers):
+        sum_copies[d - 1].wait()
+        total = total + got1[d].astype(f32)
+    scaled_t[own, :] = lax.dot_general(
+        total,
+        factor_ref[...],
+        (((1,), (1,)), ((), ())),
+        precision=lax.Precision.HIGHEST,
+        preferred_element_type=f32,
+    ).astype(bf16)
+    gather_copies = []
+    for d in range(1, peers):
+        copy = pltpu.make_async_remote_copy(
+            src_ref=scaled_t.at[own],
+            dst_ref=scaled_t.at[own],
+            send_sem=gather_send.at[d],
+            recv_sem=gather_recv.at[d],
+            device_id=in_plane(d)[1],
+            device_id_type=MESH,
+        )
+        copy.start()
+        gather_copies.append(copy)
+
+    fill(FILLS[0], FILLS[1])
+
+    for copy in gather_copies:
+        copy.wait()
+
+    def rotate(before, vectors):
+        change = lax.dot_general(
+            vectors, scaled_t[...], (((1,), (1,)), ((), ())), preferred_element_type=f32
+        )
+        return (before.astype(f32) - change).astype(bf16)
+
+    span = capacity * TILE
+    tile_copies = []
+    here = pl.ds(pl.multiple_of(me * span, span), span)
+    for d in list(range(1, peers)) + [0]:
+        peer, where = in_plane(d)
+        at = pl.ds(pl.multiple_of(peer * span, span), span)
+        outbox[d] = rotate(picked_c[at, :], picked_r[at, :])
+        if d == 0:
+            arrived[here, :] = outbox[0]
+            continue
+        copy = pltpu.make_async_remote_copy(
+            src_ref=outbox.at[d],
+            dst_ref=arrived.at[here],
+            send_sem=tile_send.at[d],
+            recv_sem=tile_recv.at[d],
+            device_id=where,
+            device_id_type=MESH,
+        )
+        copy.start()
+        tile_copies.append(copy)
+
+    def emit(i):
+        at = pl.ds(pl.multiple_of(i * EMIT, EMIT), EMIT)
+        return pltpu.make_async_copy(rot_v.at[at], rot_hbm.at[at], emit_sem.at[i])
+
+    @pl.loop(0, emits)
+    def _(i):
+        at = pl.ds(pl.multiple_of(i * EMIT, EMIT), EMIT)
+        rot_v[at, :] = rotate(coeffs_v[at, :], refl_v[at, :])
+        emit(i).start()
+
+    done = FILLS[0] + FILLS[1]
+    fill(done, n_col * boxes - done)
+
+    for copy in tile_copies:
+        copy.wait()
+
+    lanes = lax.broadcasted_iota(jnp.int32, (LANES, LANES), 1)
+    dens_copies = []
+    for d in list(range(1, n_col)) + [0]:
+        peer, where = in_col(d)
+        tall = boxes * LANES
+        at = pl.ds(pl.multiple_of(peer * tall, tall), tall)
+        orbital = jnp.dot(phi[at, :], arrived[...], preferred_element_type=f32)
+        summed = jnp.sum(orbital * orbital, axis=1, keepdims=True)
+        spread = jnp.zeros((LANES, LANES), f32)
+        for b in range(boxes):
+            spread = jnp.where(lanes == b, summed[b * LANES : (b + 1) * LANES], spread)
+        dens_own[d] = spread.T[0:8, :]
+        if d == 0:
+            continue
+        copy = pltpu.make_async_remote_copy(
+            src_ref=dens_own.at[d],
+            dst_ref=dens_got.at[d],
+            send_sem=dens_send.at[d],
+            recv_sem=dens_recv.at[d],
+            device_id=where,
+            device_id_type=MESH,
+        )
+        copy.start()
+        dens_copies.append(copy)
+    total = dens_own[0]
+    for d in range(1, n_col):
+        dens_copies[d - 1].wait()
+        total = total + dens_got[d]
+    dens_ref[...] = total[0:boxes, :] * (1.0 / (K * TILE))
+
+    @pl.loop(0, emits)
+    def _(i):
+        emit(i).wait()
+
+
+FILLS = (4, 4)
+
+
+def fits(coeffs, reflectors, atom_pos, point_pos, send_tiles, sizes):
+    n_row, n_box, n_col = sizes
+    peers = n_row * n_box
+    rows, width = coeffs.shape
+    boxes = point_pos.shape[1]
+    slots = peers * send_tiles.shape[2]
+    return (
+        width == LANES
+        and rows % LOAD == 0
+        and rows % EMIT == 0
+        and rows * (reflectors.shape[1] + 2 * width) <= 16 << 20
+        and reflectors.shape[1] % LANES == 0
+        and width % peers == 0
+        and (width // peers) % 16 == 0
+        and boxes == 4
+        and n_col <= 8
+        and point_pos.shape[2] == LANES
+        and atom_pos.shape[1] % LANES == 0
+        and slots <= LANES
+        and n_col * boxes * slots <= 512
+        and n_col * boxes >= FILLS[0] + FILLS[1]
+    )
+
+
+def per_device(
+    coeffs,
+    reflectors,
+    factor,
+    func_exp,
+    func_atom,
+    atom_pos,
+    point_pos,
+    send_tiles,
+    box_tiles,
+    box_count,
+):
+    sizes = lax.axis_size("row"), lax.axis_size("box"), lax.axis_size("col")
+    if not fits(coeffs, reflectors, atom_pos, point_pos, send_tiles, sizes):
+        return general(
+            coeffs,
+            reflectors,
+            factor,
+            func_exp,
+            func_atom,
+            atom_pos,
+            point_pos,
+            send_tiles,
+            box_tiles,
+            box_count,
+        )
+    n_row, n_box, n_col = sizes
+    peers = n_row * n_box
+    rows, width = coeffs.shape
+    nref = reflectors.shape[1]
+    boxes = point_pos.shape[1]
+    capacity = send_tiles.shape[2]
+    slots = peers * capacity
+    f32, bf16 = jnp.float32, jnp.bfloat16
+    vmem = pl.BlockSpec(memory_space=pltpu.VMEM)
+    smem = pl.BlockSpec(memory_space=pltpu.SMEM)
+    anywhere = pl.BlockSpec(memory_space=pl.ANY)
+    dma = pltpu.SemaphoreType.DMA
+    slot_info, info, picked_c, picked_r = pl.pallas_call(
+        functools.partial(prepare, n_box),
+        out_shape=(
+            jax.ShapeDtypeStruct((slots, 8, LANES), f32),
+            jax.ShapeDtypeStruct((4 * boxes, LANES), f32),
+            jax.ShapeDtypeStruct((slots * TILE, width), bf16),
+            jax.ShapeDtypeStruct((slots * TILE, nref), bf16),
+        ),
+        in_specs=[anywhere, anywhere, vmem, vmem, vmem, vmem, smem, smem, smem],
+        out_specs=(vmem, vmem, vmem, vmem),
+        scratch_shapes=[pltpu.VMEM((slots, 8, 2 * LANES), f32), dma((2 * slots,))],
+        name="slot_functions",
+    )(
+        coeffs,
+        reflectors,
+        func_exp.reshape(-1, TILE),
+        func_atom.reshape(-1, TILE),
+        atom_pos,
+        point_pos,
+        send_tiles,
+        box_tiles,
+        box_count,
+    )
+    rotated, density = pl.pallas_call(
+        functools.partial(kernel, n_row, n_box, n_col),
+        out_shape=(
+            jax.ShapeDtypeStruct((rows, width), bf16),
+            jax.ShapeDtypeStruct((boxes, LANES), f32),
+        ),
+        in_specs=[anywhere, anywhere, vmem, vmem, vmem, vmem, vmem],
+        out_specs=(anywhere, vmem),
+        scratch_shapes=[
+            pltpu.VMEM((rows, width), bf16),
+            pltpu.VMEM((rows, nref), bf16),
+            pltpu.VMEM((rows, width), bf16),
+            pltpu.VMEM((width, nref), f32),
+            pltpu.VMEM((width, nref), bf16),
+            pltpu.VMEM((peers, width // peers, nref), bf16),
+            pltpu.VMEM((width, nref), bf16),
+            pltpu.VMEM((peers, capacity * TILE, width), bf16),
+            pltpu.VMEM((slots * TILE, width), bf16),
+            pltpu.VMEM((n_col * 16, LANES), f32),
+            pltpu.VMEM((n_col * boxes, 4, LANES, LANES), f32),
+            pltpu.VMEM((n_col * boxes * LANES, slots * TILE), bf16),
+            pltpu.VMEM((n_col, 8, LANES), f32),
+            pltpu.VMEM((n_col, 8, LANES), f32),
+            dma((2 * (rows // LOAD),)),
+            dma((rows // EMIT,)),
+            dma((n_col,)),
+            dma((n_col,)),
+            dma((peers,)),
+            dma((peers,)),
+            dma((peers,)),
+            dma((peers,)),
+            dma((peers,)),
+            dma((peers,)),
+            dma((n_col,)),
+            dma((n_col,)),
+        ],
+        compiler_params=pltpu.CompilerParams(
+            collective_id=0, has_side_effects=True, vmem_limit_bytes=48 << 20
+        ),
+        name="panel_and_density",
+    )(
+        coeffs,
+        reflectors,
+        factor,
+        slot_info,
+        info,
+        picked_c,
+        picked_r,
+    )
+    return rotated, density
+
+
 def solution(mesh):
     in_specs = (
         P(("row", "box"), "col"),

time: 197 us -> 48.4 us (0.25)
  local copies, waits for them, and re-layouts: 62.4 us -> 7.29 us
  waiting for transfers between devices: 48.7 us -> 0 us
  blocking collectives: 41.9 us -> 0 us
  Pallas kernels: 0 us -> 39.9 us
  matrix products: 22.2 us -> 0 us
  between operations: 15.6 us -> 0.67 us
  starting transfers between devices: 3.53 us -> 0 us
    gather x30 -> x0, local copies, waits for them, and re-layouts: 49.4 us -> none  [the longest x3 19.8 us: per_device(): slot_centre = atom_pos[:, func_atom[funcs]]]
    psum x1 -> x0, waiting for transfers between devices: 48.7 us -> none  [per_device(): lax.psum(panel_part.astype(jnp.bfloat16), ('row', 'box'))]
    pallas_call x0 -> x2, Pallas kernels: none -> 39.9 us  [the longest x1 34.5 us: per_device(): pl.pallas_call(functools.partial(kernel, n_row, n_box, n_col), out_shape=...]
    all_gather x2 -> x0, blocking collectives: 25 us -> none  [the longest x1 13.1 us: per_device(): points = lax.all_gather(point_pos, 'col', axis=1, tiled=True)]
    dot_general x11 -> x0, matrix products: 22.2 us -> none  [the longest x8 9.66 us: box_density(): orbital = jnp.dot(phi, block, preferred_element_type=jnp.float32)]
    unnamed x2 -> x0, blocking collectives: 16.9 us -> none
    all_to_all x1 -> x0, starting transfers between devices: 3.49 us -> none  [per_device(): lax.all_to_all(outgoing, ('row', 'box'), split_axis=0, concat_axis=0, til...]
    unnamed x27 -> x13, local copies, waits for them, and re-layouts: 9.83 us -> 7.29 us
  transfers between devices with their start and end apart: 2 -> 0, of which waited for: 1 -> 0; matrix products, arithmetic and copies ran while one was open for 20% -> 0% of each run, Pallas kernels for 0% -> 0%
where the time goes in v1:
time: 48.4 us; the launch traced here: 47.9 us
  Pallas kernels  39.9 us (82%)
  local copies, waits for them, and re-layouts  7.29 us (15%)
  between operations  0.67 us (1%)
    pallas_call x1, Pallas kernels, per_device(): pl.pallas_call(functools.partial(kernel, n_row, n_box, n_col), out_shape=...  34.5 us
    unnamed x13, local copies, waits for them, and re-layouts  7.29 us
    pallas_call x1, Pallas kernels, per_device(): pl.pallas_call(functools.partial(prepare, n_box), out_shape=(jax.ShapeDty...  5.46 us

profile of v1, /device:TPU:0, one launch (start us, length us, event | category | flops | bytes accessed | tf_op | source)
XLA Modules:
  0.0 47.9 jit_solution(15345340494735690862)
XLA Ops:
  0.6 1.4 %copy.12.send_ref = s32[8,8,2]{2,1,0:T(8,128)} copy(s32[8,8,2]{1,2,0:T(2,128)} %param.17) | data formatting | bytes 1024 | tf_op args[7]
  2.0 0.0 copy-start.2
  2.0 5.5 %slot_functions.1 = (f32[16,8,128]{2,1,0:T(8,128)}, f32[16,128]{1,0:T(8,128)}, bf16[2048,128]{1,0:T(8,128)(2,1)}, bf16[2048,256]{1,0:T(8,128)(2,1)}) custom-call(bf16[10240,128]{1,0:T(8,128)(2,1)} %coeffs_hbm.3, bf16[10240,256]{1,0:T(8,128)(2,1)} %refl_hbm.3, f32[640,128]{1,0:T(8,128)} %bitcast.2, s32[640,128]{1,0:T(8,128)} %bitcast.3, f32[3,8192]{1,0:T(4,128)} %pos_ref.1, ...), custom_call_target="tpu_custom_call" | custom-call | tf_op jit(solution)/shard_map/slot_functions/pallas_call | solution.py:484
  7.5 0.0 copy-done.2
  7.5 0.0 copy-start
  7.5 1.2 %copy-done = bf16[2048,256]{1,0:T(8,128)(2,1)S(1)} copy-done((bf16[2048,256]{1,0:T(8,128)(2,1)S(1)}, bf16[2048,256]{1,0:T(8,128)(2,1)}, u32[]{:S(2)}) %copy-start) | copy-done | bytes 1048600
  8.8 0.0 copy-start.1
  8.8 1.0 %copy-done.1 = bf16[2048,128]{1,0:T(8,128)(2,1)S(1)} copy-done((bf16[2048,128]{1,0:T(8,128)(2,1)S(1)}, bf16[2048,128]{1,0:T(8,128)(2,1)}, u32[]{:S(2)}) %copy-start.1) | copy-done | bytes 524312
  9.8 0.0 copy-start.3
  9.8 0.8 %copy-done.3 = f32[16,8,128]{2,1,0:T(8,128)S(1)} copy-done((f32[16,8,128]{2,1,0:T(8,128)S(1)}, f32[16,8,128]{2,1,0:T(8,128)}, u32[]{:S(2)}) %copy-start.3) | copy-done | bytes 65560
  10.6 0.0 copy-start.4
  10.6 0.7 %copy-done.4 = f32[16,128]{1,0:T(8,128)S(1)} copy-done((f32[16,128]{1,0:T(8,128)S(1)}, f32[16,128]{1,0:T(8,128)}, u32[]{:S(2)}) %copy-start.4) | copy-done | bytes 8216
  11.3 34.5 %panel_and_density.1 = (bf16[10240,128]{1,0:T(8,128)(2,1)S(1)}, f32[4,128]{1,0:T(4,128)S(1)}) custom-call(bf16[10240,128]{1,0:T(8,128)(2,1)} %coeffs_hbm.3, bf16[10240,256]{1,0:T(8,128)(2,1)} %refl_hbm.3, f32[256,256]{1,0:T(8,128)S(1)} %copy-done.2, f32[16,8,128]{2,1,0:T(8,128)S(1)} %copy-done.3, f32[16,128]{1,0:T(8,128)S(1)} %copy-done.4, ...), custom_call_target="tpu_custom_call" | custom-call | tf_op jit(solution)/shard_map/panel_and_density/pallas_call | solution.py:507
  45.8 1.5 %copy.15 = bf16[10240,128]{1,0:T(8,128)(2,1)} copy(bf16[10240,128]{1,0:T(8,128)(2,1)S(1)} %get-tuple-element.12) | data formatting | bytes 5242880
  47.3 0.6 %copy.16 = f32[4,128]{1,0:T(4,128)} copy(f32[4,128]{1,0:T(4,128)S(1)} %get-tuple-element.13) | data formatting | bytes 4096
Async XLA Ops:
  2.0 5.5 %copy-start.2 = (f32[256,256]{1,0:T(8,128)S(1)}, f32[256,256]{1,0:T(8,128)}, u32[]{:S(2)}) copy-start(f32[256,256]{1,0:T(8,128)} %factor_ref.1) | copy-start | bytes 786436
  7.5 1.2 %copy-start = (bf16[2048,256]{1,0:T(8,128)(2,1)S(1)}, bf16[2048,256]{1,0:T(8,128)(2,1)}, u32[]{:S(2)}) copy-start(bf16[2048,256]{1,0:T(8,128)(2,1)} %get-tuple-element.9.picked_r) | copy-start | bytes 3145732
  8.8 1.0 %copy-start.1 = (bf16[2048,128]{1,0:T(8,128)(2,1)S(1)}, bf16[2048,128]{1,0:T(8,128)(2,1)}, u32[]{:S(2)}) copy-start(bf16[2048,128]{1,0:T(8,128)(2,1)} %get-tuple-element.8.picked_c) | copy-start | bytes 1572868
  9.8 0.8 %copy-start.3 = (f32[16,8,128]{2,1,0:T(8,128)S(1)}, f32[16,8,128]{2,1,0:T(8,128)}, u32[]{:S(2)}) copy-start(f32[16,8,128]{2,1,0:T(8,128)} %get-tuple-element.6.slot_info) | copy-start | bytes 196612
  10.6 0.7 %copy-start.4 = (f32[16,128]{1,0:T(8,128)S(1)}, f32[16,128]{1,0:T(8,128)}, u32[]{:S(2)}) copy-start(f32[16,128]{1,0:T(8,128)} %get-tuple-element.7.info_ref) | copy-start | bytes 24580

commit v2 on v1

--- a/solution.py
+++ b/solution.py
@@ -101,73 +101,20 @@
 EMIT = 1024
 
 
-def prepare(
-    n_box, coeffs_hbm, refl_hbm, alpha_ref, atom_ref, pos_ref, point_ref, send_ref, list_ref,
-    count_ref, slot_info, info_ref, picked_c, picked_r, window, pick_sem
-):
-    f32 = jnp.float32
-    me = lax.axis_index("row") * n_box + lax.axis_index("box")
-    slots, capacity = slot_info.shape[0], send_ref.shape[2]
-    boxes = list_ref.shape[0]
-    tiles = coeffs_hbm.shape[0] // TILE
-
-    def picks(s):
-        tile = send_ref[me, s // capacity, s % capacity]
-        source = pl.ds(pl.multiple_of(tile * TILE, TILE), TILE)
-        target = pl.ds(s * TILE, TILE)
-        return (
-            pltpu.make_async_copy(coeffs_hbm.at[source], picked_c.at[target], pick_sem.at[2 * s]),
-            pltpu.make_async_copy(refl_hbm.at[source], picked_r.at[target], pick_sem.at[2 * s + 1]),
-        )
-
-    for s in range(slots):
-        for copy in picks(s):
-            copy.start()
-
-    lane = lax.broadcasted_iota(jnp.int32, (1, LANES), 1)
-    info = [point_ref[c] for c in range(3)]
-    for b in range(boxes):
-        live = jnp.zeros((1, LANES), f32)
-        for i in range(list_ref.shape[1]):
-            used = jnp.where(i < count_ref[b], list_ref[b, i], -1)
-            live = jnp.where(lane == used, 1.0, live)
-        info.append(live)
-    info_ref[...] = jnp.concatenate(info, axis=0)
-
-    window[...] = jnp.zeros_like(window)
-    last = pos_ref.shape[1] // LANES - 1
-    depth = lax.broadcasted_iota(jnp.int32, (2 * LANES, LANES), 0)
-
-    for s in range(slots):
-        q, j = s // capacity, s % capacity
-        tile = q * tiles + send_ref[q, me, j]
-        atoms = atom_ref[pl.ds(tile, 1), :]
-        block = jnp.min(atoms) // LANES
-        after = jnp.minimum(block + 1, last)
-        window[s, 0:3, 0:LANES] = pos_ref[:, pl.ds(pl.multiple_of(block * LANES, LANES), LANES)]
-        window[s, 0:3, LANES:] = pos_ref[:, pl.ds(pl.multiple_of(after * LANES, LANES), LANES)]
-        pick = jnp.where(depth == atoms - block * LANES, 1.0, 0.0)
-        slot_info[s, 0:8, :] = jnp.dot(
-            window[s], pick, precision=lax.Precision.HIGHEST, preferred_element_type=f32
-        )
-        slot_info[s, 3:4, :] = -alpha_ref[pl.ds(tile, 1), :]
-
-    for s in range(slots):
-        for copy in picks(s):
-            copy.wait()
-
-
 def kernel(
     n_row,
     n_box,
     n_col,
     coeffs_hbm,
     refl_hbm,
-    factor_ref,
-    slot_info,
-    info_ref,
-    picked_c,
-    picked_r,
+    factor_hbm,
+    alpha_hbm,
+    atom_hbm,
+    pos_hbm,
+    point_ref,
+    send_ref,
+    list_ref,
+    count_ref,
     rot_hbm,
     dens_ref,
     coeffs_v,
@@ -181,9 +128,17 @@
     arrived,
     box_info,
     planes,
+    window,
+    slot_info,
     phi,
     dens_own,
     dens_got,
+    factor_v,
+    alpha_ref,
+    atom_ref,
+    pos_ref,
+    centres,
+    table_sem,
     load_sem,
     emit_sem,
     info_send,
@@ -201,16 +156,17 @@
     peers = n_row * n_box
     row, box, col = lax.axis_index("row"), lax.axis_index("box"), lax.axis_index("col")
     me = row * n_box + box
-    rows, width = coeffs_v.shape
+    tiles, _, width = coeffs_v.shape
+    rows = tiles * TILE
     loads = rows // LOAD
     emits = rows // EMIT
     share = width // peers
-    slots = slot_info.shape[0]
-    capacity = slots // peers
+    slots, capacity = slot_info.shape[0], send_ref.shape[1]
     boxes = dens_ref.shape[0]
+    step = LOAD // TILE
 
     def load(i):
-        at = pl.ds(i * LOAD, LOAD)
+        at = pl.ds(i * step, step)
         return (
             pltpu.make_async_copy(coeffs_hbm.at[at], coeffs_v.at[at], load_sem.at[2 * i]),
             pltpu.make_async_copy(refl_hbm.at[at], refl_v.at[at], load_sem.at[2 * i + 1]),
@@ -219,6 +175,20 @@
     for i in range(loads):
         for copy in load(i):
             copy.start()
+
+    tables = [
+        pltpu.make_async_copy(source, target, table_sem.at[i])
+        for i, (source, target) in enumerate(
+            [
+                (atom_hbm, atom_ref),
+                (alpha_hbm, alpha_ref),
+                (pos_hbm, pos_ref),
+                (factor_hbm, factor_v),
+            ]
+        )
+    ]
+    for copy in tables:
+        copy.start()
 
     def in_plane(d):
         peer = lax.rem(me + d, peers)
@@ -235,7 +205,15 @@
         pl.semaphore_signal(barrier, inc=1, device_id=in_col(d)[1], device_id_type=MESH)
 
     mine = pl.ds(pl.multiple_of(col * 16, 16), 16)
-    box_info[mine, :] = info_ref[...]
+    lane = lax.broadcasted_iota(jnp.int32, (1, LANES), 1)
+    info = [point_ref[c] for c in range(3)]
+    for b in range(boxes):
+        live = jnp.zeros((1, LANES), f32)
+        for i in range(list_ref.shape[1]):
+            used = jnp.where(i < count_ref[b], list_ref[b, i], -1)
+            live = jnp.where(lane == used, 1.0, live)
+        info.append(live)
+    box_info[mine, :] = jnp.concatenate(info, axis=0)
 
     pl.semaphore_wait(barrier, peers - 1 + n_col - 1)
 
@@ -258,9 +236,12 @@
     def _(i):
         for copy in load(i):
             copy.wait()
-        at = pl.ds(pl.multiple_of(i * LOAD, LOAD), LOAD)
+        at = pl.ds(i * step, step)
         part_f[...] += lax.dot_general(
-            coeffs_v[at, :], refl_v[at, :], (((0,), (0,)), ((), ())), preferred_element_type=f32
+            coeffs_v[at].reshape(LOAD, width),
+            refl_v[at].reshape(LOAD, refl_v.shape[2]),
+            (((0,), (0,)), ((), ())),
+            preferred_element_type=f32,
         )
 
     part_b[...] = part_f[...].astype(bf16)
@@ -278,6 +259,30 @@
         copy.start()
         sum_copies.append(copy)
 
+    for copy in tables:
+        copy.wait()
+    window[...] = jnp.zeros_like(window)
+    centres[...] = jnp.zeros_like(centres)
+    for i in range(pos_ref.shape[1] // LANES):
+        centres[i, 0:3, :] = pos_ref[:, i * LANES : (i + 1) * LANES]
+    last = pos_ref.shape[1] // LANES - 1
+    depth = lax.broadcasted_iota(jnp.int32, (2 * LANES, LANES), 0)
+
+    @pl.loop(0, slots)
+    def _(s):
+        q = s // capacity
+        tile = q * tiles + send_ref[q, lax.rem(s, capacity), me]
+        atoms = atom_ref[pl.ds(tile, 1), :]
+        block = jnp.min(atoms) // LANES
+        after = jnp.minimum(block + 1, last)
+        window[:, 0:LANES] = centres[block]
+        window[:, LANES:] = centres[after]
+        pick = jnp.where(depth == atoms - block * LANES, 1.0, 0.0)
+        slot_info[s, 0:8, :] = jnp.dot(
+            window[...], pick, precision=lax.Precision.HIGHEST, preferred_element_type=f32
+        )
+        slot_info[s, 3:4, :] = -alpha_ref[pl.ds(tile, 1), :]
+
     for copy in info_copies:
         copy.wait()
     turned = jnp.concatenate(
@@ -315,7 +320,7 @@
         total = total + got1[d].astype(f32)
     scaled_t[own, :] = lax.dot_general(
         total,
-        factor_ref[...],
+        factor_v[...],
         (((1,), (1,)), ((), ())),
         precision=lax.Precision.HIGHEST,
         preferred_element_type=f32,
@@ -349,8 +354,9 @@
     here = pl.ds(pl.multiple_of(me * span, span), span)
     for d in list(range(1, peers)) + [0]:
         peer, where = in_plane(d)
-        at = pl.ds(pl.multiple_of(peer * span, span), span)
-        outbox[d] = rotate(picked_c[at, :], picked_r[at, :])
+        for j in range(capacity):
+            tile = send_ref[me, j, peer]
+            outbox[d, j * TILE : (j + 1) * TILE, :] = rotate(coeffs_v[tile], refl_v[tile])
         if d == 0:
             arrived[here, :] = outbox[0]
             continue
@@ -372,7 +378,10 @@
     @pl.loop(0, emits)
     def _(i):
         at = pl.ds(pl.multiple_of(i * EMIT, EMIT), EMIT)
-        rot_v[at, :] = rotate(coeffs_v[at, :], refl_v[at, :])
+        some = pl.ds(i * (EMIT // TILE), EMIT // TILE)
+        rot_v[at, :] = rotate(
+            coeffs_v[some].reshape(EMIT, width), refl_v[some].reshape(EMIT, refl_v.shape[2])
+        )
         emit(i).start()
 
     done = FILLS[0] + FILLS[1]
@@ -479,42 +488,20 @@
     f32, bf16 = jnp.float32, jnp.bfloat16
     vmem = pl.BlockSpec(memory_space=pltpu.VMEM)
     smem = pl.BlockSpec(memory_space=pltpu.SMEM)
+    hbm = pl.BlockSpec(memory_space=pltpu.HBM)
     anywhere = pl.BlockSpec(memory_space=pl.ANY)
     dma = pltpu.SemaphoreType.DMA
-    slot_info, info, picked_c, picked_r = pl.pallas_call(
-        functools.partial(prepare, n_box),
-        out_shape=(
-            jax.ShapeDtypeStruct((slots, 8, LANES), f32),
-            jax.ShapeDtypeStruct((4 * boxes, LANES), f32),
-            jax.ShapeDtypeStruct((slots * TILE, width), bf16),
-            jax.ShapeDtypeStruct((slots * TILE, nref), bf16),
-        ),
-        in_specs=[anywhere, anywhere, vmem, vmem, vmem, vmem, smem, smem, smem],
-        out_specs=(vmem, vmem, vmem, vmem),
-        scratch_shapes=[pltpu.VMEM((slots, 8, 2 * LANES), f32), dma((2 * slots,))],
-        name="slot_functions",
-    )(
-        coeffs,
-        reflectors,
-        func_exp.reshape(-1, TILE),
-        func_atom.reshape(-1, TILE),
-        atom_pos,
-        point_pos,
-        send_tiles,
-        box_tiles,
-        box_count,
-    )
     rotated, density = pl.pallas_call(
         functools.partial(kernel, n_row, n_box, n_col),
         out_shape=(
             jax.ShapeDtypeStruct((rows, width), bf16),
             jax.ShapeDtypeStruct((boxes, LANES), f32),
         ),
-        in_specs=[anywhere, anywhere, vmem, vmem, vmem, vmem, vmem],
+        in_specs=[hbm] * 6 + [vmem, smem, smem, smem],
         out_specs=(anywhere, vmem),
         scratch_shapes=[
-            pltpu.VMEM((rows, width), bf16),
-            pltpu.VMEM((rows, nref), bf16),
+            pltpu.VMEM((rows // TILE, TILE, width), bf16),
+            pltpu.VMEM((rows // TILE, TILE, nref), bf16),
             pltpu.VMEM((rows, width), bf16),
             pltpu.VMEM((width, nref), f32),
             pltpu.VMEM((width, nref), bf16),
@@ -524,9 +511,17 @@
             pltpu.VMEM((slots * TILE, width), bf16),
             pltpu.VMEM((n_col * 16, LANES), f32),
             pltpu.VMEM((n_col * boxes, 4, LANES, LANES), f32),
+            pltpu.VMEM((8, 2 * LANES), f32),
+            pltpu.VMEM((slots, 8, LANES), f32),
             pltpu.VMEM((n_col * boxes * LANES, slots * TILE), bf16),
             pltpu.VMEM((n_col, 8, LANES), f32),
             pltpu.VMEM((n_col, 8, LANES), f32),
+            pltpu.VMEM(factor.shape, f32),
+            pltpu.VMEM((func_exp.shape[0] // TILE, TILE), f32),
+            pltpu.VMEM((func_exp.shape[0] // TILE, TILE), jnp.int32),
+            pltpu.VMEM(atom_pos.shape, f32),
+            pltpu.VMEM((atom_pos.shape[1] // LANES, 8, LANES), f32),
+            dma((4,)),
             dma((2 * (rows // LOAD),)),
             dma((rows // EMIT,)),
             dma((n_col,)),
@@ -541,17 +536,20 @@
             dma((n_col,)),
         ],
         compiler_params=pltpu.CompilerParams(
-            collective_id=0, has_side_effects=True, vmem_limit_bytes=48 << 20
+            collective_id=0, has_side_effects=True, vmem_limit_bytes=63 << 20
         ),
         name="panel_and_density",
     )(
-        coeffs,
-        reflectors,
+        coeffs.reshape(-1, TILE, width),
+        reflectors.reshape(-1, TILE, nref),
         factor,
-        slot_info,
-        info,
-        picked_c,
-        picked_r,
+        func_exp.reshape(-1, TILE),
+        func_atom.reshape(-1, TILE),
+        atom_pos,
+        point_pos,
+        jnp.swapaxes(send_tiles, 1, 2),
+        box_tiles,
+        box_count,
     )
     return rotated, density
 

time: 48.4 us -> 45.9 us (0.948)
  local copies, waits for them, and re-layouts: 7.29 us -> 3.48 us
  Pallas kernels: 39.9 us -> 41.5 us
    pallas_call x1, Pallas kernels: 34.5 us -> 41.5 us  [per_device(): pl.pallas_call(functools.partial(kernel, n_row, n_box, n_col), out_shape=...]
    pallas_call x1 -> x0, Pallas kernels: 5.46 us -> none  [per_device(): pl.pallas_call(functools.partial(prepare, n_box), out_shape=(jax.ShapeDty...]
    unnamed x13 -> x4, local copies, waits for them, and re-layouts: 7.29 us -> 3.48 us
where the time goes in v2:
time: 45.9 us; the launch traced here: 45.7 us
  Pallas kernels  41.5 us (90%)
  local copies, waits for them, and re-layouts  3.48 us (8%)
  between operations  0.65 us (1%)
    pallas_call x1, Pallas kernels, per_device(): pl.pallas_call(functools.partial(kernel, n_row, n_box, n_col), out_shape=...  41.5 us
    unnamed x4, local copies, waits for them, and re-layouts  3.48 us

profile of v2, /device:TPU:0, one launch (start us, length us, event | category | flops | bytes accessed | tf_op | source)
XLA Modules:
  0.0 45.7 jit_solution(17006981916441916059)
XLA Ops:
  0.6 41.5 %panel_and_density.1 = (bf16[10240,128]{1,0:T(8,128)(2,1)}, f32[4,128]{1,0:T(4,128)}) custom-call(bf16[80,128,128]{2,1,0:T(8,128)(2,1)} %bitcast.6, bf16[80,128,256]{2,1,0:T(8,128)(2,1)} %bitcast.5, f32[256,256]{1,0:T(8,128)} %factor_hbm.1, f32[640,128]{1,0:T(8,128)} %bitcast.7, s32[640,128]{1,0:T(8,128)} %bitcast.8, f32[3,8192]{1,0:T(4,128)} %pos_hbm.1, ...), custom_call_target="tpu_custom_call" | custom-call | tf_op jit(solution)/shard_map/panel_and_density/pallas_call | solution.py:494
  42.2 0.0 copy-start
  42.2 2.9 %copy.14 = bf16[10240,128]{1,0:T(8,128)(2,1)} copy(bf16[10240,128]{1,0:T(8,128)(2,1)} %get-tuple-element.4) | data formatting | bytes 5242880
  45.1 0.0 copy-done
  45.1 0.6 %copy.15 = f32[4,128]{1,0:T(4,128)} copy(f32[4,128]{1,0:T(4,128)S(1)} %copy-done) | data formatting | bytes 4096
Async XLA Ops:
  42.2 2.9 %copy-start = (f32[4,128]{1,0:T(4,128)S(1)}, f32[4,128]{1,0:T(4,128)}, u32[]{:S(2)}) copy-start(f32[4,128]{1,0:T(4,128)} %get-tuple-element.5) | copy-start | bytes 6148

commit v3 on v2

--- a/solution.py
+++ b/solution.py
@@ -133,6 +133,7 @@
     phi,
     dens_own,
     dens_got,
+    orbitals,
     factor_v,
     alpha_ref,
     atom_ref,
@@ -215,20 +216,30 @@
         info.append(live)
     box_info[mine, :] = jnp.concatenate(info, axis=0)
 
-    pl.semaphore_wait(barrier, peers - 1 + n_col - 1)
-
-    info_copies = []
-    for d in range(1, n_col):
-        copy = pltpu.make_async_remote_copy(
-            src_ref=box_info.at[mine],
-            dst_ref=box_info.at[mine],
-            send_sem=info_send.at[d],
-            recv_sem=info_recv.at[d],
-            device_id=in_col(d)[1],
-            device_id_type=MESH,
-        )
-        copy.start()
-        info_copies.append(copy)
+    for copy in tables:
+        copy.wait()
+    centres[...] = jnp.zeros_like(centres)
+    for i in range(pos_ref.shape[1] // LANES):
+        centres[i, 0:3, :] = pos_ref[:, i * LANES : (i + 1) * LANES]
+    last = pos_ref.shape[1] // LANES - 1
+    depth = lax.broadcasted_iota(jnp.int32, (2 * LANES, LANES), 0)
+
+    for s in range(slots):
+        q = s // capacity
+        tile = q * tiles + send_ref[q, s % capacity, me]
+        atoms = atom_ref[pl.ds(tile, 1), :]
+        block = jnp.min(atoms) // LANES
+        after = jnp.minimum(block + 1, last)
+        window[s, :, 0:LANES] = centres[block]
+        window[s, :, LANES:] = centres[after]
+        pick = jnp.where(depth == atoms - block * LANES, 1.0, 0.0).astype(bf16)
+        whole = window[s]
+        high = whole.astype(bf16).astype(f32)
+        middle = (whole - high).astype(bf16).astype(f32)
+        split = jnp.concatenate([high, middle, whole - high - middle], axis=0).astype(bf16)
+        three = jnp.dot(split, pick, preferred_element_type=f32)
+        slot_info[s, 0:8, :] = three[0:8] + three[8:16] + three[16:24]
+        slot_info[s, 3:4, :] = -alpha_ref[pl.ds(tile, 1), :]
 
     part_f[...] = jnp.zeros_like(part_f)
 
@@ -243,6 +254,8 @@
             (((0,), (0,)), ((), ())),
             preferred_element_type=f32,
         )
+
+    pl.semaphore_wait(barrier, peers - 1 + n_col - 1)
 
     part_b[...] = part_f[...].astype(bf16)
     sum_copies = []
@@ -259,40 +272,30 @@
         copy.start()
         sum_copies.append(copy)
 
-    for copy in tables:
-        copy.wait()
-    window[...] = jnp.zeros_like(window)
-    centres[...] = jnp.zeros_like(centres)
-    for i in range(pos_ref.shape[1] // LANES):
-        centres[i, 0:3, :] = pos_ref[:, i * LANES : (i + 1) * LANES]
-    last = pos_ref.shape[1] // LANES - 1
-    depth = lax.broadcasted_iota(jnp.int32, (2 * LANES, LANES), 0)
-
-    @pl.loop(0, slots)
-    def _(s):
-        q = s // capacity
-        tile = q * tiles + send_ref[q, lax.rem(s, capacity), me]
-        atoms = atom_ref[pl.ds(tile, 1), :]
-        block = jnp.min(atoms) // LANES
-        after = jnp.minimum(block + 1, last)
-        window[:, 0:LANES] = centres[block]
-        window[:, LANES:] = centres[after]
-        pick = jnp.where(depth == atoms - block * LANES, 1.0, 0.0)
-        slot_info[s, 0:8, :] = jnp.dot(
-            window[...], pick, precision=lax.Precision.HIGHEST, preferred_element_type=f32
-        )
-        slot_info[s, 3:4, :] = -alpha_ref[pl.ds(tile, 1), :]
-
-    for copy in info_copies:
-        copy.wait()
-    turned = jnp.concatenate(
-        [box_info[...], jnp.zeros((LANES - box_info.shape[0], LANES), f32)], axis=0
-    ).T
-    for j in range(n_col):
+    info_copies = []
+    for d in range(1, n_col):
+        copy = pltpu.make_async_remote_copy(
+            src_ref=box_info.at[mine],
+            dst_ref=box_info.at[mine],
+            send_sem=info_send.at[d],
+            recv_sem=info_recv.at[d],
+            device_id=in_col(d)[1],
+            device_id_type=MESH,
+        )
+        copy.start()
+        info_copies.append(copy)
+
+    def spread(j, block):
         for b in range(boxes):
             for c in range(4):
-                k = j * 16 + c * boxes + b
-                planes[j * boxes + b, c] = jnp.broadcast_to(turned[:, k : k + 1], (LANES, LANES))
+                k = c * boxes + b
+                planes[j * boxes + b, c] = jnp.broadcast_to(block[:, k : k + 1], (LANES, LANES))
+
+    def turn(j):
+        at = pl.ds(pl.multiple_of(j * 16, 16), 16)
+        return jnp.concatenate([box_info[at, :], jnp.zeros((LANES - 16, LANES), f32)], axis=0).T
+
+    spread(col, turn(col))
 
     def fill(first, count):
         @pl.loop(first, first + count)
@@ -311,7 +314,7 @@
                 value = jnp.where(planes[n, 3, pl.ds(s, 1), :] > 0.0, value, 0.0)
                 phi[at, pl.ds(pl.multiple_of(s * LANES, LANES), LANES)] = value.astype(bf16)
 
-    fill(0, FILLS[0])
+    fill(col * boxes, boxes)
 
     own = pl.ds(pl.multiple_of(me * share, share), share)
     total = part_f[own, :]
@@ -338,7 +341,13 @@
         copy.start()
         gather_copies.append(copy)
 
-    fill(FILLS[0], FILLS[1])
+    def fill_col(d):
+        info_copies[d - 1].wait()
+        peer = lax.rem(col + n_col - d, n_col)
+        spread(peer, turn(peer))
+        fill(peer * boxes, boxes)
+
+    fill_col(1)
 
     for copy in gather_copies:
         copy.wait()
@@ -384,11 +393,22 @@
         )
         emit(i).start()
 
-    done = FILLS[0] + FILLS[1]
-    fill(done, n_col * boxes - done)
-
-    for copy in tile_copies:
-        copy.wait()
+    for d in range(2, n_col):
+        fill_col(d)
+
+    def add(q, first):
+        deep = pl.ds(pl.multiple_of(q * span, span), span)
+
+        @pl.loop(0, n_col)
+        def _(j):
+            at = pl.ds(pl.multiple_of(j * boxes * LANES, LANES), boxes * LANES)
+            part = jnp.dot(phi[at, deep], arrived[deep, :], preferred_element_type=f32)
+            orbitals[at, :] = part if first else orbitals[at, :] + part
+
+    add(me, True)
+    for d in range(1, peers):
+        tile_copies[d - 1].wait()
+        add(lax.rem(me + peers - d, peers), False)
 
     lanes = lax.broadcasted_iota(jnp.int32, (LANES, LANES), 1)
     dens_copies = []
@@ -396,12 +416,12 @@
         peer, where = in_col(d)
         tall = boxes * LANES
         at = pl.ds(pl.multiple_of(peer * tall, tall), tall)
-        orbital = jnp.dot(phi[at, :], arrived[...], preferred_element_type=f32)
+        orbital = orbitals[at, :]
         summed = jnp.sum(orbital * orbital, axis=1, keepdims=True)
-        spread = jnp.zeros((LANES, LANES), f32)
+        turned = jnp.zeros((LANES, LANES), f32)
         for b in range(boxes):
-            spread = jnp.where(lanes == b, summed[b * LANES : (b + 1) * LANES], spread)
-        dens_own[d] = spread.T[0:8, :]
+            turned = jnp.where(lanes == b, summed[b * LANES : (b + 1) * LANES], turned)
+        dens_own[d] = turned.T[0:8, :]
         if d == 0:
             continue
         copy = pltpu.make_async_remote_copy(
@@ -423,9 +443,6 @@
     @pl.loop(0, emits)
     def _(i):
         emit(i).wait()
-
-
-FILLS = (4, 4)
 
 
 def fits(coeffs, reflectors, atom_pos, point_pos, send_tiles, sizes):
@@ -448,7 +465,7 @@
         and atom_pos.shape[1] % LANES == 0
         and slots <= LANES
         and n_col * boxes * slots <= 512
-        and n_col * boxes >= FILLS[0] + FILLS[1]
+        and n_col >= 2
     )
 
 
@@ -511,11 +528,12 @@
             pltpu.VMEM((slots * TILE, width), bf16),
             pltpu.VMEM((n_col * 16, LANES), f32),
             pltpu.VMEM((n_col * boxes, 4, LANES, LANES), f32),
-            pltpu.VMEM((8, 2 * LANES), f32),
+            pltpu.VMEM((slots, 8, 2 * LANES), f32),
             pltpu.VMEM((slots, 8, LANES), f32),
             pltpu.VMEM((n_col * boxes * LANES, slots * TILE), bf16),
             pltpu.VMEM((n_col, 8, LANES), f32),
             pltpu.VMEM((n_col, 8, LANES), f32),
+            pltpu.VMEM((n_col * boxes * LANES, width), f32),
             pltpu.VMEM(factor.shape, f32),
             pltpu.VMEM((func_exp.shape[0] // TILE, TILE), f32),
             pltpu.VMEM((func_exp.shape[0] // TILE, TILE), jnp.int32),

time: 45.9 us -> 46.6 us (1.015)
  Pallas kernels: 41.5 us -> 42.2 us
    pallas_call x1, Pallas kernels: 41.5 us -> 42.2 us  [per_device(): pl.pallas_call(functools.partial(kernel, n_row, n_box, n_col), out_shape=...]
where the time goes in v3:
time: 46.6 us; the launch traced here: 46.3 us
  Pallas kernels  42.2 us (91%)
  local copies, waits for them, and re-layouts  3.48 us (7%)
  between operations  0.65 us (1%)
    pallas_call x1, Pallas kernels, per_device(): pl.pallas_call(functools.partial(kernel, n_row, n_box, n_col), out_shape=...  42.2 us
    unnamed x4, local copies, waits for them, and re-layouts  3.48 us

profile of v3, /device:TPU:0, one launch (start us, length us, event | category | flops | bytes accessed | tf_op | source)
XLA Modules:
  0.0 46.3 jit_solution(12939448538156375989)
XLA Ops:
  0.6 42.2 %panel_and_density.1 = (bf16[10240,128]{1,0:T(8,128)(2,1)}, f32[4,128]{1,0:T(4,128)}) custom-call(bf16[80,128,128]{2,1,0:T(8,128)(2,1)} %bitcast.6, bf16[80,128,256]{2,1,0:T(8,128)(2,1)} %bitcast.5, f32[256,256]{1,0:T(8,128)} %factor_hbm.1, f32[640,128]{1,0:T(8,128)} %bitcast.7, s32[640,128]{1,0:T(8,128)} %bitcast.8, f32[3,8192]{1,0:T(4,128)} %pos_hbm.1, ...), custom_call_target="tpu_custom_call" | custom-call | tf_op jit(solution)/shard_map/panel_and_density/pallas_call | solution.py:511
  42.9 0.0 copy-start
  42.9 2.9 %copy.14 = bf16[10240,128]{1,0:T(8,128)(2,1)} copy(bf16[10240,128]{1,0:T(8,128)(2,1)} %get-tuple-element.4) | data formatting | bytes 5242880
  45.8 0.0 copy-done
  45.8 0.6 %copy.15 = f32[4,128]{1,0:T(4,128)} copy(f32[4,128]{1,0:T(4,128)S(1)} %copy-done) | data formatting | bytes 4096
Async XLA Ops:
  42.9 2.9 %copy-start = (f32[4,128]{1,0:T(4,128)S(1)}, f32[4,128]{1,0:T(4,128)}, u32[]{:S(2)}) copy-start(f32[4,128]{1,0:T(4,128)} %get-tuple-element.5) | copy-start | bytes 6148

commit v4 on v3

--- a/solution.py
+++ b/solution.py
@@ -111,10 +111,10 @@
     alpha_hbm,
     atom_hbm,
     pos_hbm,
-    point_ref,
-    send_ref,
-    list_ref,
-    count_ref,
+    point_hbm,
+    send_hbm,
+    list_hbm,
+    count_hbm,
     rot_hbm,
     dens_ref,
     coeffs_v,
@@ -133,6 +133,10 @@
     phi,
     dens_own,
     dens_got,
+    point_ref,
+    send_ref,
+    list_ref,
+    count_ref,
     orbitals,
     factor_v,
     alpha_ref,
@@ -181,6 +185,10 @@
         pltpu.make_async_copy(source, target, table_sem.at[i])
         for i, (source, target) in enumerate(
             [
+                (point_hbm, point_ref),
+                (list_hbm, list_ref),
+                (count_hbm, count_ref),
+                (send_hbm, send_ref),
                 (atom_hbm, atom_ref),
                 (alpha_hbm, alpha_ref),
                 (pos_hbm, pos_ref),
@@ -205,6 +213,8 @@
     for d in range(1, n_col):
         pl.semaphore_signal(barrier, inc=1, device_id=in_col(d)[1], device_id_type=MESH)
 
+    for copy in tables[:3]:
+        copy.wait()
     mine = pl.ds(pl.multiple_of(col * 16, 16), 16)
     lane = lax.broadcasted_iota(jnp.int32, (1, LANES), 1)
     info = [point_ref[c] for c in range(3)]
@@ -216,7 +226,7 @@
         info.append(live)
     box_info[mine, :] = jnp.concatenate(info, axis=0)
 
-    for copy in tables:
+    for copy in tables[3:]:
         copy.wait()
     centres[...] = jnp.zeros_like(centres)
     for i in range(pos_ref.shape[1] // LANES):
@@ -504,7 +514,6 @@
     slots = peers * capacity
     f32, bf16 = jnp.float32, jnp.bfloat16
     vmem = pl.BlockSpec(memory_space=pltpu.VMEM)
-    smem = pl.BlockSpec(memory_space=pltpu.SMEM)
     hbm = pl.BlockSpec(memory_space=pltpu.HBM)
     anywhere = pl.BlockSpec(memory_space=pl.ANY)
     dma = pltpu.SemaphoreType.DMA
@@ -514,7 +523,7 @@
             jax.ShapeDtypeStruct((rows, width), bf16),
             jax.ShapeDtypeStruct((boxes, LANES), f32),
         ),
-        in_specs=[hbm] * 6 + [vmem, smem, smem, smem],
+        in_specs=[hbm] * 10,
         out_specs=(anywhere, vmem),
         scratch_shapes=[
             pltpu.VMEM((rows // TILE, TILE, width), bf16),
@@ -533,13 +542,17 @@
             pltpu.VMEM((n_col * boxes * LANES, slots * TILE), bf16),
             pltpu.VMEM((n_col, 8, LANES), f32),
             pltpu.VMEM((n_col, 8, LANES), f32),
+            pltpu.VMEM(point_pos.shape, f32),
+            pltpu.SMEM((peers, capacity, peers), jnp.int32),
+            pltpu.SMEM(box_tiles.shape, jnp.int32),
+            pltpu.SMEM(box_count.shape, jnp.int32),
             pltpu.VMEM((n_col * boxes * LANES, width), f32),
             pltpu.VMEM(factor.shape, f32),
             pltpu.VMEM((func_exp.shape[0] // TILE, TILE), f32),
             pltpu.VMEM((func_exp.shape[0] // TILE, TILE), jnp.int32),
             pltpu.VMEM(atom_pos.shape, f32),
             pltpu.VMEM((atom_pos.shape[1] // LANES, 8, LANES), f32),
-            dma((4,)),
+            dma((8,)),
             dma((2 * (rows // LOAD),)),
             dma((rows // EMIT,)),
             dma((n_col,)),

time: 46.6 us -> 45.6 us (0.979)
  Pallas kernels: 42.2 us -> 41.3 us
    pallas_call x1, Pallas kernels: 42.2 us -> 41.3 us  [per_device(): pl.pallas_call(functools.partial(kernel, n_row, n_box, n_col), out_shape=...]
where the time goes in v4:
time: 45.6 us; the launch traced here: 45.4 us
  Pallas kernels  41.3 us (91%)
  local copies, waits for them, and re-layouts  3.48 us (8%)
  between operations  0.65 us (1%)
    pallas_call x1, Pallas kernels, per_device(): pl.pallas_call(functools.partial(kernel, n_row, n_box, n_col), out_shape=...  41.3 us
    unnamed x4, local copies, waits for them, and re-layouts  3.48 us

profile of v4, /device:TPU:0, one launch (start us, length us, event | category | flops | bytes accessed | tf_op | source)
XLA Modules:
  0.0 45.4 jit_solution(16538232957377393040)
XLA Ops:
  0.6 41.3 %panel_and_density.1 = (bf16[10240,128]{1,0:T(8,128)(2,1)}, f32[4,128]{1,0:T(4,128)}) custom-call(bf16[80,128,128]{2,1,0:T(8,128)(2,1)} %bitcast.6, bf16[80,128,256]{2,1,0:T(8,128)(2,1)} %bitcast.5, f32[256,256]{1,0:T(8,128)} %factor_hbm.1, f32[640,128]{1,0:T(8,128)} %bitcast.7, s32[640,128]{1,0:T(8,128)} %bitcast.8, f32[3,8192]{1,0:T(4,128)} %pos_hbm.1, ...), custom_call_target="tpu_custom_call" | custom-call | tf_op jit(solution)/shard_map/panel_and_density/pallas_call | solution.py:520
  41.9 0.0 copy-start
  42.0 2.9 %copy.14 = bf16[10240,128]{1,0:T(8,128)(2,1)} copy(bf16[10240,128]{1,0:T(8,128)(2,1)} %get-tuple-element.4) | data formatting | bytes 5242880
  44.8 0.0 copy-done
  44.9 0.6 %copy.15 = f32[4,128]{1,0:T(4,128)} copy(f32[4,128]{1,0:T(4,128)S(1)} %copy-done) | data formatting | bytes 4096
Async XLA Ops:
  41.9 2.9 %copy-start = (f32[4,128]{1,0:T(4,128)S(1)}, f32[4,128]{1,0:T(4,128)}, u32[]{:S(2)}) copy-start(f32[4,128]{1,0:T(4,128)} %get-tuple-element.5) | copy-start | bytes 6148
